TPU v7x, 32 devices: a whole 2x2x4 slice. The times are simulated.
32 devices in a mesh: grp: 2 (over x), wide: 16 (over z, y, core).
Axes of the slice: x: 2, y: 2, z: 4, core: 2. Of those that a mesh axis runs over, the one named last changes fastest.
Arguments:
- hidden_in: bfloat16 [128, 4096], P(('grp', 'wide')), parts along dimension 0, may hold values from -6 to 6
- ffn_gain: float32 [4096], replicated, may hold values from 0.1 to 1.9
- gate_weight: bfloat16 [4096, 14336], P(None, 'wide'), may hold values from -0.09375 to 0.09375
- up_weight: bfloat16 [4096, 14336], P(None, 'wide'), may hold values from -0.09375 to 0.09375
- down_weight: bfloat16 [14336, 4096], P('wide'), may hold values from -0.046875 to 0.046875
- final_gain: float32 [4096], replicated, may hold values from 0.1 to 1.9
- codes: bfloat16 [256, 128, 4096], P(('grp', 'wide')), parts along dimension 0, may hold values from -1 to 1
- scales: float32 [256, 128, 32], P(('grp', 'wide')), parts along dimension 0, may hold values from 0.5 to 5
- counts: int32 [256], P('grp'), parts along dimension 0, may hold values from 1 to 128, 10240 in all
- list_slot: int32 [256], P('grp'), parts along dimension 0, may hold values from 0 to 127, as said below
- probes: int32 [128, 8], P(('grp', 'wide')), parts along dimension 0, may hold values from 0 to 127, as said below
Outputs:
- top_scores: float32 [128, 8], P(('grp', 'wide')), parts along dimension 0
There are 2 independent parts, one for each index of `grp`. A program takes and returns all parts, laid end to end along the dimension named above; an argument that names none is the same for every part. Nothing has to cross between parts.
Inputs may be any that keep to these rules, and one draw needn't show every extreme that they name: Each query names 8 different lists. List l is held by device list_slot[l] // 8; of the 32 probes of one device's queries at most 2 name lists held by one device, and some devices are named 2 times by the queries of every device. `list_slot`: each storage row holds exactly one list. The valid rows of a list are its first counts[l] rows; some list is full.
All inputs are finite; a program needn't handle non-finite values.
Results may differ from a plain program's by a relative error of at most 0.002.
Values may be sent and summed in bfloat16 or wider, within the bound.
No kernel may reach another device: no remote copies, remote signals or barrier semaphores. Data moves between devices by JAX's collectives and lax.ppermute only.
A program may use at most 128 MiB of HBM per device.

v0:
```python
import jax
import jax.numpy as jnp
from jax import lax
from jax.sharding import PartitionSpec as P

PROBES = 8
K_TOP = 8
floor_score = -1e30


def best_values(values, count):
    return -jnp.sort(-values, axis=-1)[..., :count]


def lookup_pairs(probe_ids, list_slot, counts, lists_dev):
    flat_ids = probe_ids.reshape(-1)
    listing = jnp.arange(list_slot.shape[0], dtype=jnp.int32)
    matches = flat_ids[:, None] == listing[None, :]
    slot_of = jnp.sum(jnp.where(matches, list_slot[None, :], 0), axis=1)
    rows_of = jnp.sum(jnp.where(matches, counts[None, :], 0), axis=1)
    return (slot_of // lists_dev, slot_of % lists_dev, rows_of)


def copy_rank(owner):
    pair_total = owner.shape[-1]
    same_owner = owner[..., :, None] == owner[..., None, :]
    position = jnp.arange(pair_total, dtype=jnp.int32)
    earlier = position[:, None] > position[None, :]
    return jnp.sum(same_owner & earlier, axis=-1)


def embed(total, final_gain):
    scaled = final_gain * total
    return (scaled * lax.rsqrt(jnp.sum(scaled * scaled, axis=-1, keepdims=True) + 1e-06)).astype(
        jnp.bfloat16
    )


def score_lists(received, codes, scales):
    pair_rows, width = received.shape
    blocks = width // 128
    stored = codes.shape[0] * codes.shape[1]
    partial_sums = jnp.einsum(
        "mbk,rbk->bmr",
        received.reshape(pair_rows, blocks, 128),
        codes.reshape(stored, blocks, 128),
        preferred_element_type=jnp.float32,
    )
    return jnp.einsum(
        "bmr,rb->mr", partial_sums, scales.reshape(stored, blocks), precision=lax.Precision.HIGHEST
    )


def answer(recv_queries, recv_meta, codes, scales):
    sources, slots, width = recv_queries.shape
    lists_dev, list_rows = (codes.shape[0], codes.shape[1])
    table = score_lists(recv_queries.reshape(sources * slots, width), codes, scales)
    table = table.reshape(sources * slots, lists_dev, list_rows)
    local = recv_meta[..., 0].reshape(-1)
    valid_rows = recv_meta[..., 1].reshape(-1)
    pick_mask = local[:, None] == jnp.arange(lists_dev, dtype=jnp.int32)[None, :]
    picked = jnp.sum(jnp.where(pick_mask[:, :, None], table, 0.0), axis=1)
    alive = jnp.arange(list_rows, dtype=jnp.int32)[None, :] < valid_rows[:, None]
    masked = jnp.where(alive, picked, floor_score)
    kept = masked.reshape(sources, slots, list_rows)
    return lax.all_to_all(kept, "wide", split_axis=0, concat_axis=0, tiled=True)


def body(
    hidden_in,
    ffn_gain,
    gate_weight,
    up_weight,
    down_weight,
    final_gain,
    codes,
    scales,
    counts,
    list_slot,
    probes,
):
    q_dev, width = hidden_in.shape
    wide_count = lax.axis_size("wide")
    lists_dev = codes.shape[0]
    pair_total = q_dev * PROBES
    capacity = (pair_total + wide_count - 1) // wide_count
    own_rows = hidden_in.astype(jnp.float32)
    rows = lax.all_gather(hidden_in, "wide", axis=0, tiled=True).astype(jnp.float32)
    normed = (
        rows * lax.rsqrt(jnp.mean(rows * rows, axis=-1, keepdims=True) + 1e-05) * ffn_gain
    ).astype(jnp.bfloat16)
    gate = jnp.dot(normed, gate_weight, preferred_element_type=jnp.float32)
    upward = jnp.dot(normed, up_weight, preferred_element_type=jnp.float32)
    activated = (jax.nn.silu(gate) * upward).astype(jnp.bfloat16)
    owner, local, valid_rows = lookup_pairs(probes, list_slot, counts, lists_dev)
    target = owner * capacity + copy_rank(owner)
    mine = lax.psum_scatter(
        jnp.dot(activated, down_weight, preferred_element_type=jnp.float32),
        "wide",
        scatter_dimension=0,
        tiled=True,
    )
    embedded = embed(own_rows + mine, final_gain)
    slot_ids = jnp.arange(wide_count * capacity, dtype=jnp.int32)
    placing = slot_ids[:, None] == target[None, :]
    pair_vectors = jnp.repeat(embedded, PROBES, axis=0)
    send_queries = jnp.dot(
        placing.astype(jnp.bfloat16), pair_vectors, preferred_element_type=jnp.float32
    ).astype(jnp.bfloat16)
    send_queries = send_queries.reshape(wide_count, capacity, width)
    pair_meta = jnp.stack([local, valid_rows], axis=1)
    send_meta = jnp.sum(jnp.where(placing[:, :, None], pair_meta[None, :, :], 0), axis=1).reshape(
        wide_count, capacity, 2
    )
    returned = answer(
        lax.all_to_all(send_queries, "wide", split_axis=0, concat_axis=0, tiled=True),
        lax.all_to_all(send_meta, "wide", split_axis=0, concat_axis=0, tiled=True),
        codes,
        scales,
    )
    flat_back = returned.reshape(wide_count * capacity, returned.shape[-1])
    per_pair = jnp.take(flat_back, target, axis=0).reshape(q_dev, -1)
    return best_values(per_pair, K_TOP)


def solution(mesh):
    in_specs = (
        P(("grp", "wide"), None),
        P(),
        P(None, "wide"),
        P(None, "wide"),
        P("wide", None),
        P(),
        P(("grp", "wide"), None, None),
        P(("grp", "wide"), None, None),
        P("grp"),
        P("grp"),
        P(("grp", "wide"), None),
    )
    out_specs = P(("grp", "wide"), None)
    return jax.shard_map(body, mesh=mesh, in_specs=in_specs, out_specs=out_specs, check_vma=False)
```

profile of v0, /device:TPU:0, one launch (start us, length us, event | category | flops | bytes accessed | tf_op | source)
XLA Modules:
  0.0 191.7 jit_solution(12854098284234946222)
XLA Ops:
  6.5 0.0 copy-start
  6.5 0.0 all-reduce.3.cloned.1.call-start
  6.5 24.9 %all-gather = bf16[16,4,4096]{2,1,0:T(4,128)(2,1)S(1)} all-gather(bf16[1,4,4096]{2,1,0:T(4,128)(2,1)} %bitcast.60), channel_id=1, replica_groups=mesh['grp'=2,'wide'=16] {'wide'}, dimensions={0}, use_global_device_ids=true | all-gather | bytes 557056 | tf_op jit(solution)/shard_map/all_gather | solution.py:88
  31.5 0.1 reshape.240
  31.6 0.2 multiply_reduce_fusion.1
  31.7 4.5 %fusion.24 = f32[64,896]{1,0:T(8,128)S(1)} fusion(bf16[4096,896]{1,0:T(8,128)(2,1)} %param.13, f32[64,4096]{1,0:T(8,128)S(1)} %reshape.240, f32[4096]{0:T(1024)} %param.12, f32[64]{0:T(128)S(1)} %add_rsqrt_fusion.1), kind=kOutput, calls=%fused_computation.69 | convolution fusion | flops 470548480 | bytes 8634624 | tf_op jit(solution)/shard_map/dot_general | solution.py:92
  36.3 0.0 copy-start.4
  36.3 0.0 copy-start.5
  36.3 0.0 copy-start.6
  36.3 0.0 copy-start.7
  36.3 0.0 copy-start.1
  36.3 0.0 copy-start.2
  36.3 9.0 %fusion.5 = f32[64,4096]{1,0:T(8,128)} fusion(bf16[896,4096]{1,0:T(8,128)(2,1)} %param.15, bf16[4096,896]{1,0:T(8,128)(2,1)} %param.14, f32[64,896]{1,0:T(8,128)S(1)} %fusion.24, f32[64,4096]{1,0:T(8,128)S(1)} %reshape.240, f32[4096]{0:T(1024)S(1)} %copy-done.3, f32[64]{0:T(128)S(1)} %add_rsqrt_fusion.1), kind=kOutput, calls=%fused_computation.9 | convolution fusion | flops 940654592 | bytes 17023232 | tf_op jit(solution)/shard_map/dot_general | solution.py:98
  45.4 0.0 all-reduce.3.cloned.1.call-update
  45.4 0.1 eq.74
  45.5 0.0 copy-done.6
  45.5 0.2 select_reduce_fusion.1
  45.7 0.2 convert_reduce_fusion
  45.9 0.1 select_reduce_fusion
  46.1 0.1 reshape.223
  46.1 0.6 copy.32
  46.8 3.5 %all-to-all-start = ((s32[16,2,2]{1,2,0:T(2,128)}), s32[16,2,2]{1,2,0:T(2,128)S(1)}, u32[]{:S(2)}, u32[]{:S(2)}) async-start(s32[16,2,2]{1,2,0:T(2,128)} %copy.32), calls=%async_computation | async-start | bytes 32768 | tf_op jit(solution)/shard_map/all_to_all | solution.py:117
  50.3 0.1 reduce_sum.76
  50.4 0.1 reduce_sum.74
  50.4 0.6 dynamic-slice
  51.7 0.0 copy-done
  51.7 85.2 %all-reduce.3.cloned.1.call-done = f32[64,4096]{1,0:T(8,128)} async-done(((f32[64,4096]{1,0:T(8,128)}), f32[64,4096]{1,0:T(8,128)}) %all-reduce.3.cloned.1.call-update) | async-done | bytes 1048592
  137.0 0.0 copy-done.1
  137.0 1.1 multiply_reduce_fusion.2
  138.0 1.0 multiply_convert_fusion.1
  139.0 0.2 convolution_convert_fusion
  139.2 0.9 reshape.225
  140.1 0.0 all-to-all-done
  140.1 3.8 %all-to-all-start.1 = ((bf16[16,2,4096]{2,1,0:T(2,128)(2,1)}), bf16[16,2,4096]{2,1,0:T(2,128)(2,1)S(1)}, u32[]{:S(2)}, u32[]{:S(2)}) async-start(bf16[16,2,4096]{2,1,0:T(2,128)(2,1)} %reshape.225), calls=%async_computation.1 | async-start | bytes 524288 | tf_op jit(solution)/shard_map/all_to_all | solution.py:116
  143.9 0.1 broadcast_bitcast_fusion
  144.0 9.4 %copy.47 = bf16[128,8,32,128]{3,2,1,0:T(8,128)(2,1)} copy(bf16[128,8,32,128]{3,1,2,0:T(8,128)(2,1)} %bitcast.57) | data formatting | bytes 16777216
  153.5 0.1 eq.84
  153.6 0.1 iota_compare_fusion
  153.6 0.3 all-to-all-done.1
  153.9 0.2 reshape_reshape.3
  154.2 12.5 %multiply_reduce_fusion = f32[1024,32]{0,1:T(8,128)S(1)} fusion(bf16[1024,32,128]{2,1,0:T(8,128)(2,1)} %bitcast.58, f32[1024,32]{0,1:T(8,128)S(1)} %copy_bitcast_fusion, bf16[32,32,128]{2,1,0:T(8,128)(2,1)S(1)} %reshape_reshape.3), kind=kOutput, calls=%fused_computation.4 | convolution fusion | flops 270499840 | bytes 8912896 | tf_op jit(solution)/shard_map/mbk,rbk->bmr/dot_general | solution.py:43
  166.7 0.1 fusion.13
  166.9 0.7 compare_select_fusion
  167.5 5.7 %all-to-all-start.2 = ((f32[16,2,128]{2,1,0:T(2,128)}), f32[16,2,128]{2,1,0:T(2,128)S(1)}, u32[]{:S(2)}, u32[]{:S(2)}) async-start(f32[16,2,128]{2,1,0:T(2,128)} %compare_select_fusion), calls=%async_computation.2 | async-start | bytes 32768 | tf_op jit(solution)/shard_map/all_to_all | solution.py:66
  173.3 6.5 %all-to-all-done.2 = f32[16,2,128]{2,1,0:T(2,128)S(1)} async-done(((f32[16,2,128]{2,1,0:T(2,128)}), f32[16,2,128]{2,1,0:T(2,128)S(1)}, u32[]{:S(2)}, u32[]{:S(2)}) %all-to-all-start.2) | async-done | bytes 16416 | tf_op jit(solution)/shard_map/all_to_all | solution.py:66
  179.8 0.6 gather_fusion
  180.4 3.9 %sort_prefixfusion = f32[4,8]{1,0:T(4,128)S(1)} fusion(f32[4,1024]{1,0:T(4,128)S(1)} %select_negate_fusion), kind=kCustom, calls=%sort.15.sort_prefix | custom fusion | flops 49152 | bytes 16512 | tf_op jit(solution)/shard_map/jit(sort)/sort | solution.py:12
  184.3 0.6 neg.12
  (20 shorter events, 0.2 us)
Async XLA Ops:
  6.5 45.2 %copy-start = (f32[8,128,32]{1,2,0:T(8,128)S(1)}, f32[8,128,32]{1,2,0:T(8,128)}, u32[]{:S(2)}) copy-start(f32[8,128,32]{1,2,0:T(8,128)} %param.18) | copy-start | bytes 393220
  6.5 29.7 %copy-start.3 = (f32[4096]{0:T(1024)S(1)}, f32[4096]{0:T(1024)}, u32[]{:S(2)}) copy-start(f32[4096]{0:T(1024)} %param.12) | copy-start | bytes 49156
  6.5 130.4 %all-reduce.3.cloned.1.call-start = ((), (), s32[]{:S(2)}) async-start(), calls=%async_computation.3 | async-start | bytes 2097152
  36.3 9.1 %copy-start.4 = (s32[4,8]{1,0:T(4,128)S(1)}, s32[4,8]{1,0:T(4,128)}, u32[]{:S(2)}) copy-start(s32[4,8]{1,0:T(4,128)} %param.21) | copy-start | bytes 388
  36.3 9.2 %copy-start.5 = (s32[128]{0:T(128)S(1)}, s32[128]{0:T(128)}, u32[]{:S(2)}) copy-start(s32[128]{0:T(128)} %param.19) | copy-start | bytes 1540
  36.3 9.2 %copy-start.6 = (s32[128]{0:T(128)S(1)}, s32[128]{0:T(128)}, u32[]{:S(2)}) copy-start(s32[128]{0:T(128)} %param.20) | copy-start | bytes 1540
  36.3 14.1 %copy-start.7 = (u32[32]{0:T(128)S(1)}, u32[32]{0:T(128)}, u32[]{:S(2)}) copy-start(u32[32]{0:T(128)} %constant.80) | copy-start | bytes 388
  36.3 100.6 %copy-start.1 = (bf16[4,4096]{1,0:T(4,128)(2,1)S(1)}, bf16[4,4096]{1,0:T(4,128)(2,1)}, u32[]{:S(2)}) copy-start(bf16[4,4096]{1,0:T(4,128)(2,1)} %param.11) | copy-start | bytes 98308
  36.3 100.6 %copy-start.2 = (f32[4096]{0:T(1024)S(1)}, f32[4096]{0:T(1024)}, u32[]{:S(2)}) copy-start(f32[4096]{0:T(1024)} %param.16) | copy-start | bytes 49156
  46.8 93.4 %all-to-all-start = ((s32[16,2,2]{1,2,0:T(2,128)}), s32[16,2,2]{1,2,0:T(2,128)S(1)}, u32[]{:S(2)}, u32[]{:S(2)}) async-start(s32[16,2,2]{1,2,0:T(2,128)} %copy.32), calls=%async_computation | async-start | bytes 32768 | tf_op jit(solution)/shard_map/all_to_all | solution.py:117
  140.1 13.8 %all-to-all-start.1 = ((bf16[16,2,4096]{2,1,0:T(2,128)(2,1)}), bf16[16,2,4096]{2,1,0:T(2,128)(2,1)S(1)}, u32[]{:S(2)}, u32[]{:S(2)}) async-start(bf16[16,2,4096]{2,1,0:T(2,128)(2,1)} %reshape.225), calls=%async_computation.1 | async-start | bytes 524288 | tf_op jit(solution)/shard_map/all_to_all | solution.py:116
  167.5 12.2 %all-to-all-start.2 = ((f32[16,2,128]{2,1,0:T(2,128)}), f32[16,2,128]{2,1,0:T(2,128)S(1)}, u32[]{:S(2)}, u32[]{:S(2)}) async-start(f32[16,2,128]{2,1,0:T(2,128)} %compare_select_fusion), calls=%async_computation.2 | async-start | bytes 32768 | tf_op jit(solution)/shard_map/all_to_all | solution.py:66
Sparse Core Ops, SparseCore 0:
  45.5 91.3 all-reduce.2
where the time goes:
time: 192 us
  waiting for transfers between devices  92 us (48%)
  matrix products  26.3 us (14%)
  blocking collectives  24.9 us (13%)
  between operations  14.3 us (7%)
  local copies, waits for them, and re-layouts  13 us (7%)
  starting transfers between devices  13 us (7%)
  other arithmetic  8.15 us (4%)
    unnamed x2, waiting for transfers between devices  85.2 us
    all_gather x1, blocking collectives, body(): lax.all_gather(hidden_in, 'wide', axis=0, tiled=True).astype(jnp.float32)  24.9 us
    dot_general x1, matrix products, score_lists(): jnp.einsum('mbk,rbk->bmr', received.reshape(pair_rows, blocks, 128), code...  12.5 us
    unnamed x20, local copies, waits for them, and re-layouts  10.2 us
    dot_general x1, matrix products, body(): jnp.dot(activated, down_weight, preferred_element_type=jnp.float32)  9.03 us
    all_to_all x1, waiting for transfers between devices, answer(): return lax.all_to_all(kept, 'wide', split_axis=0, concat_axis=0, tiled=True)  6.49 us
    all_to_all x1, starting transfers between devices, answer(): return lax.all_to_all(kept, 'wide', split_axis=0, concat_axis=0, tiled=True)  5.72 us
    dot_general x1, matrix products, body(): gate = jnp.dot(normed, gate_weight, preferred_element_type=jnp.float32)  4.51 us
  transfers between devices with their start and end apart: 4, of which 3 were waited for; matrix products, arithmetic and copies ran while one was open for 8% of the time, Pallas kernels for 0%

commit v1 on v0

--- a/solution.py
+++ b/solution.py
@@ -1,11 +1,38 @@
+import functools
 import jax
 import jax.numpy as jnp
 from jax import lax
 from jax.sharding import PartitionSpec as P
+from jax.lax import axis_index, axis_size, ppermute
 
 PROBES = 8
 K_TOP = 8
 floor_score = -1e30
+
+
+def _review_slices(x0, in_dim):
+    x0 = jnp.moveaxis(x0, 0, in_dim)
+    met_up = x0.shape
+    return x0.reshape(*met_up[:in_dim], met_up[in_dim] * met_up[in_dim + 1], *met_up[in_dim + 2 :])
+
+
+def _state_lots_all(shard_in, a_name):
+    n_shards = axis_size(a_name)
+    finding = shard_in[None]
+    for pp in range(n_shards.bit_length() - 1):
+        b_now = 1 << pp
+        low = ppermute(finding, a_name, perm=tuple(((d, d ^ b_now) for d in range(n_shards))))
+        newest = jnp.stack([finding, low], axis=0)
+        block_last = axis_index(a_name) >> pp & 1
+        finding = jnp.where(block_last == 0, newest, newest[::-1]).reshape(-1, *shard_in.shape)
+    return finding
+
+
+def bring_the_hubs(content, u, dim_k):
+    return _review_slices(_state_lots_all(content, u), dim_k)
+
+
+finish_slices_up = functools.partial(bring_the_hubs, u="wide", dim_k=0)
 
 
 def best_values(values, count):
@@ -85,7 +112,7 @@
     pair_total = q_dev * PROBES
     capacity = (pair_total + wide_count - 1) // wide_count
     own_rows = hidden_in.astype(jnp.float32)
-    rows = lax.all_gather(hidden_in, "wide", axis=0, tiled=True).astype(jnp.float32)
+    rows = finish_slices_up(hidden_in).astype(jnp.float32)
     normed = (
         rows * lax.rsqrt(jnp.mean(rows * rows, axis=-1, keepdims=True) + 1e-05) * ffn_gain
     ).astype(jnp.bfloat16)

time: 192 us -> 200 us (1.042)
  blocking collectives: 24.9 us -> 0 us
  waiting for transfers between devices: 92 us -> 111 us
  starting transfers between devices: 13 us -> 22.6 us
  other arithmetic: 8.15 us -> 11 us
    all_gather x1 -> x0, blocking collectives: 24.9 us -> none  [body(): lax.all_gather(hidden_in, 'wide', axis=0, tiled=True).astype(jnp.float32)]
    ppermute x0 -> x4, waiting for transfers between devices: none -> 17.4 us  [_state_lots_all(): ppermute(finding, a_name, perm=tuple(((d, d ^ b_now) for d in range(n_sha...]
    ppermute x0 -> x4, starting transfers between devices: none -> 7.56 us  [_state_lots_all(): ppermute(finding, a_name, perm=tuple(((d, d ^ b_now) for d in range(n_sha...]
    unnamed x20 -> x14, local copies, waits for them, and re-layouts: 10.2 us -> 10.2 us
  transfers between devices with their start and end apart: 4 -> 8, of which waited for: 3 -> 6; matrix products, arithmetic and copies ran while one was open for 8% -> 8% of each run, Pallas kernels for 0% -> 0%
where the time goes in v1:
time: 200 us; the launch traced here: 199 us
  waiting for transfers between devices  111 us (56%)
  matrix products  26.3 us (13%)
  starting transfers between devices  22.6 us (11%)
  between operations  14.3 us (7%)
  local copies, waits for them, and re-layouts  14 us (7%)
  other arithmetic  11 us (6%)
    unnamed x2, waiting for transfers between devices  87 us
    ppermute x4, waiting for transfers between devices, _state_lots_all(): ppermute(finding, a_name, perm=tuple(((d, d ^ b_now) for d in range(n_sha...  17.4 us
    dot_general x1, matrix products, score_lists(): jnp.einsum('mbk,rbk->bmr', received.reshape(pair_rows, blocks, 128), code...  12.5 us
    unnamed x14, local copies, waits for them, and re-layouts  10.2 us
    dot_general x1, matrix products, body(): jnp.dot(activated, down_weight, preferred_element_type=jnp.float32)  9.02 us
    ppermute x4, starting transfers between devices, _state_lots_all(): ppermute(finding, a_name, perm=tuple(((d, d ^ b_now) for d in range(n_sha...  7.56 us
    all_to_all x1, waiting for transfers between devices, answer(): return lax.all_to_all(kept, 'wide', split_axis=0, concat_axis=0, tiled=True)  6.49 us
    all_to_all x1, starting transfers between devices, answer(): return lax.all_to_all(kept, 'wide', split_axis=0, concat_axis=0, tiled=True)  5.72 us
  transfers between devices with their start and end apart: 8, of which 6 were waited for; matrix products, arithmetic and copies ran while one was open for 8% of the time, Pallas kernels for 0%

profile of v1, /device:TPU:0, one launch (start us, length us, event | category | flops | bytes accessed | tf_op | source)
XLA Modules:
  0.0 199.4 jit_solution(3023043226393728042)
XLA Ops:
  6.5 0.5 collective-permute-start
  7.0 0.8 eq.86
  7.8 0.8 select_reduce_fusion.1
  8.7 0.2 convert_reduce_fusion
  8.9 0.8 pad_maximum_fusion.3
  9.7 2.6 %collective-permute-start.1 = (bf16[2,4,4096]{2,1,0:T(4,128)(2,1)S(1)}, bf16[2,4,4096]{2,1,0:T(4,128)(2,1)S(1)}, u32[]{:S(2)}, u32[]{:S(2)}) collective-permute-start(bf16[2,4,4096]{2,1,0:T(4,128)(2,1)S(1)} %get-tuple-element.12), channel_id=1, source_target_pairs={{0,2},{1,3},{2,0},{3,1},{4,6},{5,7},{6,4},{7,5},{8,10},{9,11},{10,... | collective-permute-start | bytes 196616 | tf_op jit(solution)/shard_map/ppermute | solution.py:24
  12.4 2.7 %collective-permute-done.1 = bf16[2,4,4096]{2,1,0:T(4,128)(2,1)S(1)} collective-permute-done((bf16[2,4,4096]{2,1,0:T(4,128)(2,1)S(1)}, bf16[2,4,4096]{2,1,0:T(4,128)(2,1)S(1)}, u32[]{:S(2)}, u32[]{:S(2)}) %collective-permute-start.1) | collective-permute-done | bytes 65568 | tf_op jit(solution)/shard_map/ppermute | solution.py:24
  15.1 0.1 pad_maximum_fusion.2
  15.2 1.9 collective-permute-start.2
  17.1 3.5 %collective-permute-done.2 = bf16[4,4,4096]{2,1,0:T(4,128)(2,1)S(1)} collective-permute-done((bf16[4,4,4096]{2,1,0:T(4,128)(2,1)S(1)}, bf16[4,4,4096]{2,1,0:T(4,128)(2,1)S(1)}, u32[]{:S(2)}, u32[]{:S(2)}) %collective-permute-start.2) | collective-permute-done | bytes 131104 | tf_op jit(solution)/shard_map/ppermute | solution.py:24
  20.6 0.2 pad_maximum_fusion.1
  20.8 0.1 reverse_select_fusion.1
  20.9 2.6 %collective-permute-start.3 = (bf16[8,4,4096]{2,1,0:T(4,128)(2,1)S(1)}, bf16[8,4,4096]{2,1,0:T(4,128)(2,1)S(1)}, u32[]{:S(2)}, u32[]{:S(2)}) collective-permute-start(bf16[8,4,4096]{2,1,0:T(4,128)(2,1)S(1)} %bitcast.73), channel_id=1, source_target_pairs={{0,8},{1,9},{2,10},{3,11},{4,12},{5,13},{6,14},{7,15},{8,0},{9,1},... | collective-permute-start | bytes 786440 | tf_op jit(solution)/shard_map/ppermute | solution.py:24
  23.5 11.2 %collective-permute-done.3 = bf16[8,4,4096]{2,1,0:T(4,128)(2,1)S(1)} collective-permute-done((bf16[8,4,4096]{2,1,0:T(4,128)(2,1)S(1)}, bf16[8,4,4096]{2,1,0:T(4,128)(2,1)S(1)}, u32[]{:S(2)}, u32[]{:S(2)}) %collective-permute-start.3) | collective-permute-done | bytes 262176 | tf_op jit(solution)/shard_map/ppermute | solution.py:24
  34.7 0.4 pad_maximum_fusion
  35.1 0.2 fusion.6
  35.3 0.5 multiply_reduce_fusion.1
  35.8 0.4 reshape.253
  36.2 0.1 rsqrt.20
  36.3 4.5 %fusion.27 = f32[64,896]{1,0:T(8,128)S(1)} fusion(bf16[4096,896]{1,0:T(8,128)(2,1)} %param.13, f32[64,4096]{1,0:T(8,128)S(1)} %reshape.253, f32[4096]{0:T(1024)} %param.12, f32[64]{0:T(128)S(1)} %rsqrt.20), kind=kOutput, calls=%fused_computation.80 | convolution fusion | flops 470548480 | bytes 8634624 | tf_op jit(solution)/shard_map/dot_general | solution.py:119
  40.8 9.0 %fusion.5 = f32[64,4096]{1,0:T(8,128)} fusion(bf16[896,4096]{1,0:T(8,128)(2,1)} %param.15, bf16[4096,896]{1,0:T(8,128)(2,1)} %param.14, f32[64,896]{1,0:T(8,128)S(1)} %fusion.27, f32[64,4096]{1,0:T(8,128)S(1)} %reshape.253, f32[4096]{0:T(1024)S(1)} %copy-done.3, f32[64]{0:T(128)S(1)} %rsqrt.20), kind=kOutput, calls=%fused_computation.9 | convolution fusion | flops 940654592 | bytes 17023232 | tf_op jit(solution)/shard_map/dot_general | solution.py:125
  49.9 0.1 select_reduce_fusion
  50.0 0.1 reshape.243
  50.1 0.6 copy.32
  50.7 5.5 %all-to-all-start = ((s32[16,2,2]{1,2,0:T(2,128)}), s32[16,2,2]{1,2,0:T(2,128)S(1)}, u32[]{:S(2)}, u32[]{:S(2)}) async-start(s32[16,2,2]{1,2,0:T(2,128)} %copy.32), calls=%async_computation | async-start | bytes 32768 | tf_op jit(solution)/shard_map/all_to_all | solution.py:144
  56.2 0.1 reduce_sum.76
  56.3 0.1 reduce_sum.74
  56.4 0.6 dynamic-slice
  57.6 87.0 %all-reduce.3.cloned.1.call-done = f32[64,4096]{1,0:T(8,128)} async-done(((f32[64,4096]{1,0:T(8,128)}), f32[64,4096]{1,0:T(8,128)}) %all-reduce.3.cloned.1.call-update) | async-done | bytes 1048592
  144.6 1.1 multiply_reduce_fusion.2
  145.7 1.0 multiply_convert_fusion.1
  146.7 0.2 convolution_convert_fusion
  146.9 0.9 reshape.248
  147.8 3.8 %all-to-all-start.1 = ((bf16[16,2,4096]{2,1,0:T(2,128)(2,1)}), bf16[16,2,4096]{2,1,0:T(2,128)(2,1)S(1)}, u32[]{:S(2)}, u32[]{:S(2)}) async-start(bf16[16,2,4096]{2,1,0:T(2,128)(2,1)} %reshape.248), calls=%async_computation.1 | async-start | bytes 524288 | tf_op jit(solution)/shard_map/all_to_all | solution.py:143
  151.6 0.1 broadcast_bitcast_fusion
  151.7 9.4 %copy.47 = bf16[128,8,32,128]{3,2,1,0:T(8,128)(2,1)} copy(bf16[128,8,32,128]{3,1,2,0:T(8,128)(2,1)} %bitcast.70) | data formatting | bytes 16777216
  161.2 0.1 eq.96
  161.3 0.1 iota_compare_fusion
  161.3 0.3 all-to-all-done.1
  161.6 0.2 reshape_reshape.4
  161.8 12.5 %multiply_reduce_fusion = f32[1024,32]{0,1:T(8,128)S(1)} fusion(bf16[1024,32,128]{2,1,0:T(8,128)(2,1)} %bitcast.71, f32[1024,32]{0,1:T(8,128)S(1)} %copy_bitcast_fusion, bf16[32,32,128]{2,1,0:T(8,128)(2,1)S(1)} %reshape_reshape.4), kind=kOutput, calls=%fused_computation.4 | convolution fusion | flops 270499840 | bytes 8912896 | tf_op jit(solution)/shard_map/mbk,rbk->bmr/dot_general | solution.py:70
  174.4 0.1 fusion.14
  174.6 0.7 compare_select_fusion
  175.2 5.7 %all-to-all-start.2 = ((f32[16,2,128]{2,1,0:T(2,128)}), f32[16,2,128]{2,1,0:T(2,128)S(1)}, u32[]{:S(2)}, u32[]{:S(2)}) async-start(f32[16,2,128]{2,1,0:T(2,128)} %compare_select_fusion), calls=%async_computation.2 | async-start | bytes 32768 | tf_op jit(solution)/shard_map/all_to_all | solution.py:93
  181.0 6.5 %all-to-all-done.2 = f32[16,2,128]{2,1,0:T(2,128)S(1)} async-done(((f32[16,2,128]{2,1,0:T(2,128)}), f32[16,2,128]{2,1,0:T(2,128)S(1)}, u32[]{:S(2)}, u32[]{:S(2)}) %all-to-all-start.2) | async-done | bytes 16416 | tf_op jit(solution)/shard_map/all_to_all | solution.py:93
  187.5 0.6 gather_fusion
  188.1 3.9 %sort_prefixfusion = f32[4,8]{1,0:T(4,128)S(1)} fusion(f32[4,1024]{1,0:T(4,128)S(1)} %select_negate_fusion), kind=kCustom, calls=%sort.15.sort_prefix | custom fusion | flops 49152 | bytes 16512 | tf_op jit(solution)/shard_map/jit(sort)/sort | solution.py:39
  192.0 0.6 neg.12
  (30 shorter events, 0.3 us)
Async XLA Ops:
  6.5 51.1 %copy-start = (f32[8,128,32]{1,2,0:T(8,128)S(1)}, f32[8,128,32]{1,2,0:T(8,128)}, u32[]{:S(2)}) copy-start(f32[8,128,32]{1,2,0:T(8,128)} %param.18) | copy-start | bytes 393220
  6.5 138.1 %all-reduce.3.cloned.1.call-start = ((), (), s32[]{:S(2)}) async-start(), calls=%async_computation.3 | async-start | bytes 2097152
  6.5 2.3 %collective-permute-start = (bf16[1,4,4096]{2,1,0:T(4,128)(2,1)}, bf16[1,4,4096]{2,1,0:T(4,128)(2,1)S(1)}, u32[]{:S(2)}, u32[]{:S(2)}) collective-permute-start(bf16[1,4,4096]{2,1,0:T(4,128)(2,1)} %bitcast.77), channel_id=1, source_target_pairs={{0,1},{1,0},{2,3},{3,2},{4,5},{5,4},{6,7},{7,6},{8,9},{9,8},{10,11... | collective-permute-start | bytes 98312 | tf_op jit(solution)/shard_map/ppermute | solution.py:24
  9.7 5.3 %collective-permute-start.1 = (bf16[2,4,4096]{2,1,0:T(4,128)(2,1)S(1)}, bf16[2,4,4096]{2,1,0:T(4,128)(2,1)S(1)}, u32[]{:S(2)}, u32[]{:S(2)}) collective-permute-start(bf16[2,4,4096]{2,1,0:T(4,128)(2,1)S(1)} %get-tuple-element.12), channel_id=1, source_target_pairs={{0,2},{1,3},{2,0},{3,1},{4,6},{5,7},{6,4},{7,5},{8,10},{9,11},{10,... | collective-permute-start | bytes 196616 | tf_op jit(solution)/shard_map/ppermute | solution.py:24
  15.2 5.4 %collective-permute-start.2 = (bf16[4,4,4096]{2,1,0:T(4,128)(2,1)S(1)}, bf16[4,4,4096]{2,1,0:T(4,128)(2,1)S(1)}, u32[]{:S(2)}, u32[]{:S(2)}) collective-permute-start(bf16[4,4,4096]{2,1,0:T(4,128)(2,1)S(1)} %bitcast.75), channel_id=1, source_target_pairs={{0,4},{1,5},{2,6},{3,7},{4,0},{5,1},{6,2},{7,3},{8,12},{9,13},{10,... | collective-permute-start | bytes 393224 | tf_op jit(solution)/shard_map/ppermute | solution.py:24
  20.8 20.0 %copy-start.3 = (f32[4096]{0:T(1024)S(1)}, f32[4096]{0:T(1024)}, u32[]{:S(2)}) copy-start(f32[4096]{0:T(1024)} %param.12) | copy-start | bytes 49156
  20.9 13.8 %collective-permute-start.3 = (bf16[8,4,4096]{2,1,0:T(4,128)(2,1)S(1)}, bf16[8,4,4096]{2,1,0:T(4,128)(2,1)S(1)}, u32[]{:S(2)}, u32[]{:S(2)}) collective-permute-start(bf16[8,4,4096]{2,1,0:T(4,128)(2,1)S(1)} %bitcast.73), channel_id=1, source_target_pairs={{0,8},{1,9},{2,10},{3,11},{4,12},{5,13},{6,14},{7,15},{8,0},{9,1},... | collective-permute-start | bytes 786440 | tf_op jit(solution)/shard_map/ppermute | solution.py:24
  40.8 15.6 %copy-start.4 = (u32[32]{0:T(128)S(1)}, u32[32]{0:T(128)}, u32[]{:S(2)}) copy-start(u32[32]{0:T(128)} %constant.87) | copy-start | bytes 388
  40.8 103.8 %copy-start.1 = (bf16[4,4096]{1,0:T(4,128)(2,1)S(1)}, bf16[4,4096]{1,0:T(4,128)(2,1)}, u32[]{:S(2)}) copy-start(bf16[4,4096]{1,0:T(4,128)(2,1)} %param.11) | copy-start | bytes 98308
  40.8 103.8 %copy-start.2 = (f32[4096]{0:T(1024)S(1)}, f32[4096]{0:T(1024)}, u32[]{:S(2)}) copy-start(f32[4096]{0:T(1024)} %param.16) | copy-start | bytes 49156
  50.7 97.1 %all-to-all-start = ((s32[16,2,2]{1,2,0:T(2,128)}), s32[16,2,2]{1,2,0:T(2,128)S(1)}, u32[]{:S(2)}, u32[]{:S(2)}) async-start(s32[16,2,2]{1,2,0:T(2,128)} %copy.32), calls=%async_computation | async-start | bytes 32768 | tf_op jit(solution)/shard_map/all_to_all | solution.py:144
  147.8 13.8 %all-to-all-start.1 = ((bf16[16,2,4096]{2,1,0:T(2,128)(2,1)}), bf16[16,2,4096]{2,1,0:T(2,128)(2,1)S(1)}, u32[]{:S(2)}, u32[]{:S(2)}) async-start(bf16[16,2,4096]{2,1,0:T(2,128)(2,1)} %reshape.248), calls=%async_computation.1 | async-start | bytes 524288 | tf_op jit(solution)/shard_map/all_to_all | solution.py:143
  175.2 12.2 %all-to-all-start.2 = ((f32[16,2,128]{2,1,0:T(2,128)}), f32[16,2,128]{2,1,0:T(2,128)S(1)}, u32[]{:S(2)}, u32[]{:S(2)}) async-start(f32[16,2,128]{2,1,0:T(2,128)} %compare_select_fusion), calls=%async_computation.2 | async-start | bytes 32768 | tf_op jit(solution)/shard_map/all_to_all | solution.py:93
Sparse Core Ops, SparseCore 0:
  50.0 94.5 all-reduce.2
